TPU v7x, 32 devices: a whole 2x2x4 slice. The times are simulated.
32 devices in a mesh: groups: 2 (over y), expert: 4 (over z), tensor: 2 (over x), inner: 2 (over core).
Axes of the slice: x: 2, y: 2, z: 4, core: 2. Of those that a mesh axis runs over, the one named last changes fastest.
Arguments:
- tokens: bfloat16 [1024, 7168], P(('groups', 'expert'), ('tensor', 'inner')), parts along dimension 0, may hold values from -6 to 6
- expert_ids: int32 [1024, 8], P(('groups', 'expert')), parts along dimension 0, may hold values from 0 to 31, all different within a row; in each aligned block of 128 rows (0 to 127, 128 to 255, ...) at most 96 rows name the same one
- gate_weights: float32 [1024, 8], P(('groups', 'expert')), parts along dimension 0, may hold values from 0.05 to 0.45
- base_weights: bfloat16 [3, 1024, 7168], P(None, 'expert', ('tensor', 'inner')), may hold values from -0.0625 to 0.0625
- in_factor: bfloat16 [3840, 7168], P('expert', ('tensor', 'inner')), may hold values from -0.0625 to 0.0625
- out_factors: bfloat16 [2, 3840, 1024], P(None, 'expert', ('tensor', 'inner')), may hold values from -0.375 to 0.375
- ranks: int32 [32], P('expert'), may hold values from 64 to 512, as said below
Outputs:
- mixed: bfloat16 [1024, 7168], P(('groups', 'expert'), ('tensor', 'inner')), parts along dimension 0
There are 2 independent parts, one for each index of `groups`. A program takes and returns all parts, laid end to end along the dimension named above; an argument that names none is the same for every part. Nothing has to cross between parts.
Inputs may be any that keep to these rules, and one draw needn't show every extreme that they name: `expert_ids`: in each aligned block of 128 tokens no expert is chosen more than 96 times, and some expert is chosen exactly 96 times; the experts of one token differ. The ranks of each aligned block of 8 experts sum to exactly 960.
All inputs are finite; a program needn't handle non-finite values.
Results may differ from a plain program's by a relative error of at most 0.023.
Values may be sent and summed in bfloat16 or wider, within the bound.
No kernel may reach another device: no remote copies, remote signals or barrier semaphores. Data moves between devices by JAX's collectives and lax.ppermute only.
A program may use at most 64 MiB of HBM per device.

v0:
```python
import jax
import jax.numpy as jnp
from jax import lax
from jax.sharding import PartitionSpec as P

RANK_MAX = 512


def on_device(tokens, expert_ids, gate_weights, base_weights, in_factor, out_factors, ranks):
    tok_rows, feat_slice = tokens.shape
    top_count = expert_ids.shape[1]
    owners = lax.axis_size("expert")
    local_count = ranks.shape[0]
    experts = local_count * owners
    capacity = min(tok_rows, 3 * tok_rows * top_count // experts)
    hidden_slice = out_factors.shape[2]
    width = RANK_MAX
    gathered = lax.all_gather(base_weights, "expert", axis=1, tiled=True)
    partial_value = jnp.einsum(
        "td,gfd->tgf", tokens, gathered[:2], preferred_element_type=jnp.float32
    )
    base_rows = lax.psum_scatter(
        partial_value.astype(jnp.bfloat16), ("tensor", "inner"), scatter_dimension=2, tiled=True
    )
    pairs = tok_rows * top_count
    flat_ids = expert_ids.reshape(pairs)
    columns = lax.broadcasted_iota(jnp.int32, (pairs, experts), 1)
    onehot = (flat_ids[:, None] == columns).astype(jnp.bfloat16)
    row_pos = lax.broadcasted_iota(jnp.int32, (pairs, pairs), 0)
    col_pos = lax.broadcasted_iota(jnp.int32, (pairs, pairs), 1)
    earlier = (row_pos > col_pos).astype(jnp.bfloat16)
    counts = jnp.dot(earlier, onehot, preferred_element_type=jnp.float32)
    slot = jnp.sum(counts * onehot.astype(jnp.float32), axis=1).astype(jnp.int32)
    owner_of = flat_ids // local_count
    member_of = flat_ids % local_count
    target = (member_of * owners + owner_of) * capacity + slot
    source_row = lax.broadcasted_iota(jnp.int32, (pairs,), 0) // top_count
    outgoing = jnp.zeros((local_count * owners * capacity, feat_slice), jnp.bfloat16)
    outgoing = outgoing.at[target].set(tokens[source_row])
    outgoing = outgoing.reshape(local_count, owners, capacity, feat_slice)
    arrived = lax.all_to_all(outgoing, "expert", split_axis=1, concat_axis=1, tiled=True)
    slots = owners * capacity
    arrived = arrived.reshape(local_count, slots, feat_slice)
    starts = jnp.cumsum(ranks) - ranks
    in_pad = jnp.concatenate([in_factor, jnp.zeros((width, feat_slice), jnp.bfloat16)], 0)
    out_pad = jnp.concatenate([out_factors, jnp.zeros((2, width, hidden_slice), jnp.bfloat16)], 1)
    within = lax.broadcasted_iota(jnp.int32, (1, width), 1)
    terms = []
    for member in range(local_count):
        window = lax.dynamic_slice_in_dim(in_pad, starts[member], width, 0)
        terms.append(
            lax.dot_general(
                arrived[member],
                window,
                (((1,), (1,)), ((), ())),
                preferred_element_type=jnp.float32,
            )
        )
    stacked = jnp.stack(
        [
            jnp.where(within < ranks[member], terms[member], jnp.float32(0.0))
            for member in range(local_count)
        ]
    )
    summed = lax.psum(stacked.astype(jnp.bfloat16), ("tensor", "inner"))
    latents = [summed[member] for member in range(local_count)]
    outputs = []
    for member in range(local_count):
        factor = lax.dynamic_slice_in_dim(out_pad, starts[member], width, 1)
        outputs.append(
            jnp.einsum(
                "rc,gcf->rgf", latents[member], factor, preferred_element_type=jnp.float32
            ).astype(jnp.bfloat16)
        )
    replies = jnp.stack(outputs).reshape(local_count, owners, capacity, 2, hidden_slice)
    returned = lax.all_to_all(replies, "expert", split_axis=1, concat_axis=1, tiled=True)
    returned = returned.reshape(local_count * owners * capacity, 2, hidden_slice)
    delta = returned[target].reshape(tok_rows, top_count, 2, hidden_slice)
    summed_rows = base_rows.astype(jnp.float32)[:, None] + delta.astype(jnp.float32)
    hidden = (jax.nn.silu(summed_rows[:, :, 0]) * summed_rows[:, :, 1]).astype(jnp.bfloat16)
    combined = jnp.sum(gate_weights[:, :, None] * hidden.astype(jnp.float32), axis=1).astype(
        jnp.bfloat16
    )
    full_hidden = lax.all_gather(combined, ("tensor", "inner"), axis=1, tiled=True)
    return jnp.dot(full_hidden, gathered[2], preferred_element_type=jnp.float32).astype(
        jnp.bfloat16
    )


def solution(mesh):
    return jax.shard_map(
        on_device,
        mesh=mesh,
        in_specs=(
            P(("groups", "expert"), ("tensor", "inner")),
            P(("groups", "expert"), None),
            P(("groups", "expert"), None),
            P(None, "expert", ("tensor", "inner")),
            P("expert", ("tensor", "inner")),
            P(None, "expert", ("tensor", "inner")),
            P("expert"),
        ),
        out_specs=P(("groups", "expert"), ("tensor", "inner")),
        check_vma=False,
    )
```

profile of v0, /device:TPU:0, one launch (start us, length us, event | category | flops | bytes accessed | tf_op | source)
XLA Modules:
  0.0 655.1 jit_solution(18073991329550731420)
XLA Ops:
  7.4 0.8 copy.40
  8.4 0.5 fusion.52
  9.0 31.3 %scatter_custom_fusion = bf16[3072,1792]{1,0:T(8,128)(2,1)} fusion(s32[1024]{0:T(1024)S(1)} %bitcast.155, bf16[]{:T(256)} %constant.47.clone.1, bf16[128,1792]{1,0:T(8,128)(2,1)S(1)} %copy-done, s32[1024]{0:T(1024)S(1)} %broadcast_clamp_fusion.1), kind=kCustom, calls=%fused_computation.13 | custom fusion | bytes 11010050 | tf_op jit(solution)/shard_map/scatter | solution.py:39
  40.3 9.6 %copy.42 = bf16[8,4,96,1792]{3,2,0,1:T(8,128)(2,1)} copy(bf16[8,4,96,1792]{3,2,1,0:T(8,128)(2,1)} %bitcast.135) | data formatting | bytes 22020096 | tf_op jit(solution)/shard_map/reshape | solution.py:40
  50.0 6.5 all-to-all-start
  56.6 0.7 fusion.94
  72.4 0.7 fusion.93
  73.1 0.6 iota_compare_fusion.15
  73.8 0.6 iota_compare_fusion.14
  74.4 0.6 iota_compare_fusion.13
  75.0 0.7 iota_compare_fusion.12
  75.7 0.6 iota_compare_fusion.11
  76.2 0.7 iota_compare_fusion.10
  76.9 0.6 iota_compare_fusion.9
  77.6 0.7 iota_compare_fusion.8
  78.2 218.9 %all-to-all-done = bf16[8,4,96,1792]{3,2,0,1:T(8,128)(2,1)} async-done(((bf16[8,4,96,1792]{3,2,0,1:T(8,128)(2,1)}), bf16[8,4,96,1792]{3,2,0,1:T(8,128)(2,1)}, u32[]{:S(2)}, u32[]{:S(2)}) %all-to-all-start) | async-done | bytes 11010080 | tf_op jit(solution)/shard_map/all_to_all | solution.py:41
  297.2 4.9 fusion.91
  302.4 1.9 fusion.50
  304.3 1.9 fusion.48
  306.2 1.9 fusion.46
  308.1 1.9 fusion.44
  310.0 1.9 fusion.42
  311.9 1.9 fusion.40
  313.8 1.9 fusion.38
  315.7 1.9 fusion.36
  318.2 67.2 %all-reduce.4.cloned.1.call-done = bf16[8,384,512]{2,1,0:T(8,128)(2,1)} async-done(((bf16[8,384,512]{2,1,0:T(8,128)(2,1)}), bf16[8,384,512]{2,1,0:T(8,128)(2,1)}) %all-reduce.4.cloned.1.call-update) | async-done | bytes 3145744 | tf_op jit(solution)/shard_map/psum | solution.py:65
  385.4 1.6 convolution_convert_fusion.7
  387.1 1.5 convolution_convert_fusion.6
  388.7 0.5 convolution_convert_fusion.5
  389.2 0.5 convolution_convert_fusion.4
  389.8 0.5 convolution_convert_fusion.3
  390.3 0.5 convolution_convert_fusion.2
  390.9 0.5 convolution_convert_fusion.1
  391.4 0.5 convolution_convert_fusion
  392.0 1.9 copy.54
  393.9 4.7 all-to-all-start.1
  398.6 179.9 %all-gather.2.cloned.1.call-done = bf16[3,1024,1792]{2,1,0:T(8,128)(2,1)} async-done(((bf16[3,256,1792]{2,1,0:T(8,128)(2,1)}), bf16[3,1024,1792]{2,1,0:T(8,128)(2,1)}) %all-gather.2.cloned.1.call-update) | async-done | bytes 11010064 | tf_op jit(solution)/shard_map/all_gather | solution.py:18
  578.4 6.3 fusion.16
  584.9 19.8 %reduce-scatter.2.cloned.1.call-done = bf16[128,2,256]{2,0,1:T(8,128)(2,1)} async-done(((bf16[128,2,1024]{2,0,1:T(8,128)(2,1)}), bf16[128,2,256]{2,0,1:T(8,128)(2,1)}) %reduce-scatter.2.cloned.1.call-update) | async-done | bytes 131088 | tf_op jit(solution)/shard_map/reduce_scatter | solution.py:22
  604.7 1.0 copy.39
  605.8 2.2 copy.51
  607.9 20.6 %copy.52 = bf16[3072,2,256]{2,1,0:T(2,128)(2,1)} copy(bf16[3072,2,256]{2,0,1:T(8,128)(2,1)S(1)} %bitcast.136) | data formatting | bytes 6291456 | tf_op jit(solution)/shard_map/reshape | solution.py:77
  628.5 6.1 gather_fusion
  634.6 1.3 convert_add_fusion
  635.9 1.6 fusion.92
  637.5 0.6 multiply_reduce_fusion
  638.1 5.8 all_gather.7
  643.8 3.5 fusion.7
  (36 shorter events, 1.7 us)
Async XLA Ops:
  7.4 1.7 copy-start
  50.0 6.5 copy-start.3
  50.0 247.2 %all-to-all-start = ((bf16[8,4,96,1792]{3,2,0,1:T(8,128)(2,1)}), bf16[8,4,96,1792]{3,2,0,1:T(8,128)(2,1)}, u32[]{:S(2)}, u32[]{:S(2)}) async-start(bf16[8,4,96,1792]{3,2,0,1:T(8,128)(2,1)} %copy.42), calls=%async_computation.1 | async-start | bytes 22020096 | tf_op jit(solution)/shard_map/all_to_all | solution.py:41
  56.5 329.0 %all-reduce.4.cloned.1.call-start = ((), (), s32[]{:S(2)}) async-start(), calls=%async_computation.5 | async-start | bytes 6291456 | tf_op jit(solution)/shard_map/psum | solution.py:65
  297.2 5.2 copy-start.5
  317.6 67.9 %copy-start.1 = (bf16[2,960,256]{2,1,0:T(8,128)(2,1)S(1)}, bf16[2,960,256]{2,1,0:T(8,128)(2,1)}, u32[]{:S(2)}) copy-start(bf16[2,960,256]{2,1,0:T(8,128)(2,1)} %param.12) | copy-start | bytes 2949124
  317.6 260.9 %all-gather.2.cloned.1.call-start = ((), (), s32[]{:S(2)}) async-start(), calls=%async_computation.3 | async-start | bytes 13762560 | tf_op jit(solution)/shard_map/all_gather | solution.py:18
  385.4 3.2 copy-start.2
  393.9 211.9 %all-to-all-start.1 = ((bf16[8,4,96,2,256]{4,2,0,3,1:T(8,128)(2,1)}), bf16[8,4,96,2,256]{4,2,0,3,1:T(8,128)(2,1)}, u32[]{:S(2)}, u32[]{:S(2)}) async-start(bf16[8,4,96,2,256]{4,2,0,3,1:T(8,128)(2,1)} %copy.54), calls=%async_computation.2 | async-start | bytes 6291456 | tf_op jit(solution)/shard_map/all_to_all | solution.py:76
  398.5 186.3 %copy-start.4 = (f32[128,8]{0,1:T(8,128)S(1)}, f32[128,8]{0,1:T(8,128)}, u32[]{:S(2)}) copy-start(f32[128,8]{0,1:T(8,128)} %param.9) | copy-start | bytes 12292
  398.5 206.2 %reduce-scatter.2.cloned.1.call-start = ((), (), s32[]{:S(2)}) async-start(), calls=%async_computation.4 | async-start | bytes 655360 | tf_op jit(solution)/shard_map/reduce_scatter | solution.py:22
Sparse Core Ops, SparseCore 0:
  317.7 67.6 all-reduce.3
  584.9 19.7 reduce-scatter.1
Sparse Core Ops, SparseCore 1:
  319.6 258.7 all-gather.1
where the time goes:
time: 664 us; the launch traced here: 655 us
  waiting for transfers between devices  486 us (73%)
  local copies, waits for them, and re-layouts  82.2 us (12%)
  matrix products  31.7 us (5%)
  between operations  30.7 us (5%)
  starting transfers between devices  11.4 us (2%)
  other arithmetic  7.15 us (1%)
    all_to_all x1, waiting for transfers between devices, on_device(): lax.all_to_all(outgoing, 'expert', split_axis=1, concat_axis=1, tiled=True)  219 us
    all_gather x1, waiting for transfers between devices, on_device(): gathered = lax.all_gather(base_weights, 'expert', axis=1, tiled=True)  180 us
    psum x1, waiting for transfers between devices, on_device(): summed = lax.psum(stacked.astype(jnp.bfloat16), ('tensor', 'inner'))  67.2 us
    scatter x1, local copies, waits for them, and re-layouts, on_device(): outgoing = outgoing.at[target].set(tokens[source_row])  31.3 us
    reshape x1, local copies, waits for them, and re-layouts, on_device(): returned.reshape(local_count * owners * capacity, 2, hidden_slice)  20.6 us
    reduce_scatter x1, waiting for transfers between devices, on_device(): lax.psum_scatter(partial_value.astype(jnp.bfloat16), ('tensor', 'inner'),...  19.8 us
    dot_general x8, matrix products, on_device(): lax.dot_general(arrived[member], window, (((1,), (1,)), ((), ())), prefer...  15.2 us
  transfers between devices with their start and end apart: 5, of which 4 were waited for; matrix products, arithmetic and copies ran while one was open for 3% of the time, Pallas kernels for 0%

commit v1 on v0

--- a/solution.py
+++ b/solution.py
@@ -62,7 +62,9 @@
             for member in range(local_count)
         ]
     )
-    summed = lax.psum(stacked.astype(jnp.bfloat16), ("tensor", "inner"))
+    own = stacked.astype(jnp.bfloat16)
+    parts = lax.all_gather(own, ("tensor", "inner"))
+    summed = jnp.sum(parts, axis=0)
     latents = [summed[member] for member in range(local_count)]
     outputs = []
     for member in range(local_count):

time: 664 us -> 738 us (1.11)
  waiting for transfers between devices: 486 us -> 558 us
  other arithmetic: 7.15 us -> 16.4 us
    all_gather x0 -> x1, waiting for transfers between devices: none -> 80.7 us  [on_device(): parts = lax.all_gather(own, ('tensor', 'inner'))]
    psum x1 -> x0, waiting for transfers between devices: 67.2 us -> none  [on_device(): summed = lax.psum(stacked.astype(jnp.bfloat16), ('tensor', 'inner'))]
    all_gather x1, waiting for transfers between devices: 180 us -> 238 us  [on_device(): gathered = lax.all_gather(base_weights, 'expert', axis=1, tiled=True)]
    reduce_sum x0 -> x1, other arithmetic: none -> 9.26 us  [on_device(): summed = jnp.sum(parts, axis=0)]
  transfers between devices with their start and end apart: 5 -> 5, of which waited for: 4 -> 4; matrix products, arithmetic and copies ran while one was open for 3% -> 4% of each run, Pallas kernels for 0% -> 0%
where the time goes in v1:
time: 738 us; the launch traced here: 728 us
  waiting for transfers between devices  558 us (76%)
  local copies, waits for them, and re-layouts  75.4 us (10%)
  matrix products  32 us (4%)
  between operations  28.8 us (4%)
  other arithmetic  16.4 us (2%)
  starting transfers between devices  11.6 us (2%)
    all_gather x1, waiting for transfers between devices, on_device(): gathered = lax.all_gather(base_weights, 'expert', axis=1, tiled=True)  238 us
    all_to_all x1, waiting for transfers between devices, on_device(): lax.all_to_all(outgoing, 'expert', split_axis=1, concat_axis=1, tiled=True)  219 us
    all_gather x1, waiting for transfers between devices, on_device(): parts = lax.all_gather(own, ('tensor', 'inner'))  80.7 us
    scatter x1, local copies, waits for them, and re-layouts, on_device(): outgoing = outgoing.at[target].set(tokens[source_row])  24.4 us
    reshape x1, local copies, waits for them, and re-layouts, on_device(): returned.reshape(local_count * owners * capacity, 2, hidden_slice)  20.6 us
    reduce_scatter x1, waiting for transfers between devices, on_device(): lax.psum_scatter(partial_value.astype(jnp.bfloat16), ('tensor', 'inner'),...  19.8 us
    dot_general x8, matrix products, on_device(): lax.dot_general(arrived[member], window, (((1,), (1,)), ((), ())), prefer...  15.3 us
  transfers between devices with their start and end apart: 5, of which 4 were waited for; matrix products, arithmetic and copies ran while one was open for 4% of the time, Pallas kernels for 0%

profile of v1, /device:TPU:0, one launch (start us, length us, event | category | flops | bytes accessed | tf_op | source)
XLA Modules:
  0.0 728.4 jit_solution(5765432838375914047)
XLA Ops:
  6.5 0.8 copy.40
  7.6 0.5 fusion.52
  8.2 24.4 %scatter_custom_fusion = bf16[3072,1792]{1,0:T(8,128)(2,1)} fusion(s32[1024]{0:T(1024)S(1)} %bitcast.155, bf16[]{:T(256)} %constant.48.clone.1, bf16[128,1792]{1,0:T(8,128)(2,1)S(1)} %copy-done, s32[1024]{0:T(1024)S(1)} %broadcast_clamp_fusion.1), kind=kCustom, calls=%fused_computation.13 | custom fusion | bytes 11010050 | tf_op jit(solution)/shard_map/scatter | solution.py:39
  32.6 9.6 %copy.42 = bf16[8,4,96,1792]{3,2,0,1:T(8,128)(2,1)} copy(bf16[8,4,96,1792]{3,2,1,0:T(8,128)(2,1)} %bitcast.135) | data formatting | bytes 22020096 | tf_op jit(solution)/shard_map/reshape | solution.py:40
  42.2 6.5 all-to-all-start
  48.9 0.7 fusion.94
  64.7 0.7 fusion.93
  65.4 0.6 iota_compare_fusion.15
  66.0 0.6 iota_compare_fusion.14
  66.7 0.6 iota_compare_fusion.13
  67.3 0.7 iota_compare_fusion.12
  67.9 0.6 iota_compare_fusion.11
  68.5 0.7 iota_compare_fusion.10
  69.2 0.6 iota_compare_fusion.9
  69.9 0.7 iota_compare_fusion.8
  70.5 218.9 %all-to-all-done = bf16[8,4,96,1792]{3,2,0,1:T(8,128)(2,1)} async-done(((bf16[8,4,96,1792]{3,2,0,1:T(8,128)(2,1)}), bf16[8,4,96,1792]{3,2,0,1:T(8,128)(2,1)}, u32[]{:S(2)}, u32[]{:S(2)}) %all-to-all-start) | async-done | bytes 11010080 | tf_op jit(solution)/shard_map/all_to_all | solution.py:41
  289.4 4.9 fusion.91
  294.6 1.9 fusion.50
  296.5 1.9 fusion.48
  298.4 1.9 fusion.46
  300.3 1.9 fusion.44
  302.3 1.9 fusion.42
  304.2 1.9 fusion.40
  306.1 1.9 fusion.38
  308.0 1.9 fusion.36
  310.2 0.5 all-gather.3.cloned.1.call-update
  310.7 80.7 %all-gather.5.cloned.1.call-done = bf16[4,8,384,512]{3,2,1,0:T(8,128)(2,1)} async-done(((bf16[1,8,384,512]{3,2,1,0:T(8,128)(2,1)}), bf16[4,8,384,512]{3,2,1,0:T(8,128)(2,1)}) %all-gather.5.cloned.1.call-update) | async-done | bytes 12582928 | tf_op jit(solution)/shard_map/all_gather | solution.py:66
  391.4 9.3 %reduce_sum.31 = bf16[8,384,512]{2,1,0:T(8,128)(2,1)} reduce(bf16[4,8,384,512]{3,2,1,0:T(8,128)(2,1)} %all-gather.5.cloned.1.call-done, bf16[]{:T(256)} %constant.48.clone.1), dimensions={0}, to_apply=%region_4.5 | reduce | flops 4718592 | bytes 15728642 | tf_op jit(solution)/shard_map/reduce_sum | solution.py:67
  400.7 1.7 convolution_convert_fusion.7
  402.4 1.6 convolution_convert_fusion.6
  404.1 0.5 convolution_convert_fusion.5
  404.6 0.5 convolution_convert_fusion.4
  405.2 0.5 convolution_convert_fusion.3
  406.3 0.5 convolution_convert_fusion.1
  407.4 2.0 copy.54
  409.3 4.6 all-to-all-start.1
  414.3 238.4 %all-gather.3.cloned.1.call-done = bf16[3,1024,1792]{2,1,0:T(8,128)(2,1)} async-done(((bf16[3,256,1792]{2,1,0:T(8,128)(2,1)}), bf16[3,1024,1792]{2,1,0:T(8,128)(2,1)}) %all-gather.3.cloned.1.call-update) | async-done | bytes 11010064 | tf_op jit(solution)/shard_map/all_gather | solution.py:18
  652.7 6.4 fusion.16
  659.2 19.8 %reduce-scatter.2.cloned.1.call-done = bf16[128,2,256]{2,0,1:T(8,128)(2,1)} async-done(((bf16[128,2,1024]{2,0,1:T(8,128)(2,1)}), bf16[128,2,256]{2,0,1:T(8,128)(2,1)}) %reduce-scatter.2.cloned.1.call-update) | async-done | bytes 131088 | tf_op jit(solution)/shard_map/reduce_scatter | solution.py:22
  679.0 1.0 copy.39
  680.1 2.2 copy.51
  682.2 20.6 %copy.52 = bf16[3072,2,256]{2,1,0:T(2,128)(2,1)} copy(bf16[3072,2,256]{2,0,1:T(8,128)(2,1)S(1)} %bitcast.136) | data formatting | bytes 6291456 | tf_op jit(solution)/shard_map/reshape | solution.py:79
  702.8 6.1 gather_fusion
  708.9 1.3 convert_add_fusion
  710.2 1.6 fusion.92
  711.8 0.6 multiply_reduce_fusion
  712.4 5.8 all_gather.12
  718.1 3.5 fusion.7
  (37 shorter events, 2.6 us)
Async XLA Ops:
  6.5 1.7 copy-start
  42.2 6.5 copy-start.3
  42.2 247.2 %all-to-all-start = ((bf16[8,4,96,1792]{3,2,0,1:T(8,128)(2,1)}), bf16[8,4,96,1792]{3,2,0,1:T(8,128)(2,1)}, u32[]{:S(2)}, u32[]{:S(2)}) async-start(bf16[8,4,96,1792]{3,2,0,1:T(8,128)(2,1)} %copy.42), calls=%async_computation.1 | async-start | bytes 22020096 | tf_op jit(solution)/shard_map/all_to_all | solution.py:41
  48.7 342.7 %all-gather.5.cloned.1.call-start = ((), (), s32[]{:S(2)}) async-start(), calls=%async_computation.5 | async-start | bytes 15728640 | tf_op jit(solution)/shard_map/all_gather | solution.py:66
  289.4 5.2 copy-start.5
  309.9 342.7 %all-gather.3.cloned.1.call-start = ((), (), s32[]{:S(2)}) async-start(), calls=%async_computation.3 | async-start | bytes 13762560 | tf_op jit(solution)/shard_map/all_gather | solution.py:18
  310.7 90.0 %copy-start.1 = (bf16[2,960,256]{2,1,0:T(8,128)(2,1)S(1)}, bf16[2,960,256]{2,1,0:T(8,128)(2,1)}, u32[]{:S(2)}) copy-start(bf16[2,960,256]{2,1,0:T(8,128)(2,1)} %param.12) | copy-start | bytes 2949124
  400.7 3.4 copy-start.2
  409.3 270.7 %all-to-all-start.1 = ((bf16[8,4,96,2,256]{4,2,0,3,1:T(8,128)(2,1)}), bf16[8,4,96,2,256]{4,2,0,3,1:T(8,128)(2,1)}, u32[]{:S(2)}, u32[]{:S(2)}) async-start(bf16[8,4,96,2,256]{4,2,0,3,1:T(8,128)(2,1)} %copy.54), calls=%async_computation.2 | async-start | bytes 6291456 | tf_op jit(solution)/shard_map/all_to_all | solution.py:78
  414.0 245.1 %copy-start.4 = (f32[128,8]{0,1:T(8,128)S(1)}, f32[128,8]{0,1:T(8,128)}, u32[]{:S(2)}) copy-start(f32[128,8]{0,1:T(8,128)} %param.9) | copy-start | bytes 12292
  414.0 265.0 %reduce-scatter.2.cloned.1.call-start = ((), (), s32[]{:S(2)}) async-start(), calls=%async_computation.4 | async-start | bytes 655360 | tf_op jit(solution)/shard_map/reduce_scatter | solution.py:22
Sparse Core Ops, SparseCore 0:
  310.1 81.3 all-gather.4
  393.0 259.6 all-gather.2
  659.2 19.7 reduce-scatter.1
